TPU v7x, 32 devices: a whole 2x2x4 slice. The times are simulated.
32 devices in a mesh: rows: 8 (over y, x, core), cols: 4 (over z).
Axes of the slice: x: 2, y: 2, z: 4, core: 2. Of those that a mesh axis runs over, the one named last changes fastest.
Arguments:
- white_real: float32 [4096, 4096], P('rows', 'cols'), may hold values from -6 to 6
- white_imag: float32 [4096, 4096], P('rows', 'cols'), may hold values from -6 to 6
- covariates: bfloat16 [16, 4096, 4096], P(None, 'rows', 'cols'), may hold values from -6 to 6
- coefficients: float32 [16], replicated, may hold values from -0.9 to 0.9
- counts: int32 [4096, 4096], P('rows', 'cols'), may hold values from 0 to 5
- land_mask: int32 [4096, 4096], P('rows', 'cols'), may hold values from 0 to 1
- field_hyper: float32 [2], replicated, may hold values from 1 to 2
Outputs:
- step_real: float32 [4096, 4096], P('rows', 'cols')
- step_imag: float32 [4096, 4096], P('rows', 'cols')
- coef_grad: float32 [16], replicated
- objective: float32 [], replicated
All inputs are finite; a program needn't handle non-finite values.
Results may differ from a plain program's by a relative error of at most 0.0003.
Values sent between devices are 32-bit elements; how exact they have to be, the bound alone decides.
No kernel may reach another device: no remote copies, remote signals or barrier semaphores. Data moves between devices by JAX's collectives and lax.ppermute only.
A program may use at most 128 MiB of HBM per device.

v0:
```python
import math
import jax
import jax.numpy as jnp
from jax import lax
from jax.sharding import PartitionSpec as P

NG = 4096
lasso_weight = 0.02
ridge_weight = 0.1


def field_spectrum(field_hyper, wave_row, wave_col):
    amplitude = 0.2 * field_hyper[0]
    freq_range = field_hyper[1]
    radius = (wave_row[:, None] * wave_row[:, None] + wave_col[None, :] * wave_col[None, :]) / (
        freq_range * freq_range
    )
    return amplitude * (1.0 + NG / freq_range * jnp.power(1.0 + radius, -0.75))


def angle_table(left_len, right_len, modulus):
    product = lax.iota(jnp.int32, left_len)[:, None] * lax.iota(jnp.int32, right_len)[None, :]
    angles = (product % modulus).astype(jnp.float32) * (2.0 * math.pi / modulus)
    return (jnp.cos(angles), jnp.sin(angles))


def inverse_transform(pieces, want_real):
    highest = lax.Precision.HIGHEST
    components = pieces.shape[0]
    row_count = pieces.shape[1]
    length = pieces.shape[2]
    factor = 8
    others = length // factor
    shaped = pieces.reshape(components, row_count, others, factor)
    big_cos, big_sin = angle_table(others, others, others)

    def apply_big(table, block):
        return jnp.einsum("rnm,nk->rmk", block, table, precision=highest)

    if components == 2:
        real_mid = apply_big(big_cos, shaped[0]) - apply_big(big_sin, shaped[1])
        imag_mid = apply_big(big_sin, shaped[0]) + apply_big(big_cos, shaped[1])
    else:
        real_mid = apply_big(big_cos, shaped[0])
        imag_mid = apply_big(big_sin, shaped[0])
    tw_cos, tw_sin = angle_table(factor, others, length)
    real_tw = real_mid * tw_cos - imag_mid * tw_sin
    imag_tw = real_mid * tw_sin + imag_mid * tw_cos
    small_cos, small_sin = angle_table(factor, factor, factor)

    def apply_small(table, block):
        return jnp.einsum("rmk,mj->rjk", block, table, precision=highest)

    real_out = (apply_small(small_cos, real_tw) - apply_small(small_sin, imag_tw)).reshape(
        1, row_count, length
    )
    if want_real:
        return real_out
    imag_out = (apply_small(small_sin, real_tw) + apply_small(small_cos, imag_tw)).reshape(
        1, row_count, length
    )
    return jnp.concatenate([real_out, imag_out], axis=0)


def middle_step(spread):
    returned = lax.all_to_all(spread, "cols", split_axis=2, concat_axis=1, tiled=True)
    flipped = jnp.swapaxes(returned, 1, 2)
    return lax.all_to_all(flipped, "rows", split_axis=1, concat_axis=2, tiled=True)


def grid_transform(pieces, want_real):
    full_rows = lax.all_to_all(pieces, "cols", split_axis=1, concat_axis=2, tiled=True)
    halfway = inverse_transform(full_rows, False)
    columns = middle_step(halfway)
    second = inverse_transform(columns, want_real)
    blocks_out = lax.all_to_all(second, "rows", split_axis=2, concat_axis=1, tiled=True)
    return jnp.swapaxes(blocks_out, 1, 2) * (1.0 / NG)


def shards(white_real, white_imag, covariates, coefficients, counts, land_mask, field_hyper):
    highest = lax.Precision.HIGHEST
    rows_here = white_real.shape[0]
    cols_here = white_real.shape[1]
    freq_row = lax.axis_index("rows") * rows_here + lax.iota(jnp.int32, rows_here)
    freq_col = lax.axis_index("cols") * cols_here + lax.iota(jnp.int32, cols_here)
    wave_row = jnp.minimum(freq_row, NG - freq_row).astype(jnp.float32)
    wave_col = jnp.minimum(freq_col, NG - freq_col).astype(jnp.float32)
    spectrum = field_spectrum(field_hyper, wave_row, wave_col)
    scaled = jnp.stack([spectrum * white_real, spectrum * white_imag])
    latent = grid_transform(scaled, True)[0]
    cov_full = covariates.astype(jnp.float32)
    linear = jnp.einsum("j,jrc->rc", coefficients, cov_full, precision=highest)
    log_rate = linear + latent
    intensity = jnp.exp(log_rate)
    land_vals = land_mask.astype(jnp.float32)
    count_vals = counts.astype(jnp.float32)
    residual = land_vals * (intensity - count_vals)
    partial_coef = jnp.einsum("jrc,rc->j", cov_full, residual, precision=highest)
    partial_loss = jnp.sum(land_vals * (intensity - count_vals * log_rate)) + 0.5 * jnp.sum(
        white_real * white_real + white_imag * white_imag
    )
    adjoint = grid_transform(residual[None], False)
    total_coef, total_loss = lax.psum((partial_coef, partial_loss), ("rows", "cols"))
    per_cell = 1.0 / (NG * NG)
    coef_grad = (
        total_coef * per_cell + lasso_weight * jnp.sign(coefficients) + ridge_weight * coefficients
    )
    objective = (
        total_loss * per_cell
        + lasso_weight * jnp.sum(jnp.abs(coefficients))
        + 0.5 * ridge_weight * jnp.sum(coefficients * coefficients)
    )
    curvature = 1.0 + spectrum * spectrum
    step_real = (spectrum * adjoint[0] + white_real) / curvature
    step_imag = (white_imag - spectrum * adjoint[1]) / curvature
    return (step_real, step_imag, coef_grad, objective)


def solution(mesh):
    return jax.shard_map(
        shards,
        mesh=mesh,
        in_specs=(
            P("rows", "cols"),
            P("rows", "cols"),
            P(None, "rows", "cols"),
            P(),
            P("rows", "cols"),
            P("rows", "cols"),
            P(),
        ),
        out_specs=(P("rows", "cols"), P("rows", "cols"), P(), P()),
        check_vma=False,
    )
```

profile of v0, /device:TPU:0, one launch (start us, length us, event | category | flops | bytes accessed | tf_op | source)
XLA Modules:
  0.0 896.9 jit_solution(2084490301962304620)
XLA Ops:
  4.6 3.8 multiply_bitcast_fusion
  12.1 5.8 pad_maximum_fusion
  17.9 6.5 all-to-all-start
  24.5 93.3 %all-to-all-done = f32[2,512,1024]{2,0,1:T(2,128)} async-done(((f32[2,512,1024]{2,0,1:T(2,128)}), f32[2,512,1024]{2,0,1:T(2,128)}, u32[]{:S(2)}, u32[]{:S(2)}) %all-to-all-start) | async-done | bytes 4194336 | tf_op jit(solution)/shard_map/all_to_all | solution.py:72
  117.8 3.5 copy.149
  127.4 10.3 %fusion.62 = f32[128,8,512]{2,0,1:T(8,128)} fusion(f32[128,512,8]{1,0,2:T(8,128)} %copy.151), kind=kOutput, calls=%fused_computation.88 | convolution fusion | flops 3224895488 | bytes 4194304 | tf_op jit(solution)/shard_map/rnm,nk->rmk/dot_general | solution.py:38
  137.6 8.4 fusion.74
  149.8 9.9 %convolution_subtract_fusion.2 = f32[128,8,512]{2,0,1:T(8,128)S(1)} fusion(f32[128,8,512]{2,0,1:T(8,128)} %fusion.74, f32[128,512,8]{1,0,2:T(8,128)S(1)} %copy.153), kind=kOutput, calls=%fused_computation.73 | convolution fusion | flops 3225419776 | bytes 6291456 | tf_op jit(solution)/shard_map/rnm,nk->rmk/dot_general | solution.py:38
  159.8 9.2 %multiply_subtract_fusion.3 = (f32[128,8,512]{2,0,1:T(8,128)S(1)}, f32[128,8,512]{2,0,1:T(8,128)S(1)}) fusion(f32[128,8,512]{2,0,1:T(8,128)S(1)} %convolution_subtract_fusion.2, f32[8,512]{1,0:T(8,128)S(1)} %get-tuple-element.32, f32[8,512]{1,0:T(8,128)S(1)} %get-tuple-element.33, f32[128,8,512]{2,0,1:T(8,128)S(1)} %copy-done.8, f32[128,512,8]{1,0,2:T(8,128)S(1)} %copy.153), kind=kOutput, calls=%fused_computation.41 | convolution fusion | flops 3228565504 | bytes 10518528 | tf_op jit(solution)/shard_map/rnm,nk->rmk/dot_general | solution.py:38
  177.6 4.3 add_bitcast_fusion.2
  186.9 5.3 pad_maximum_fusion.1
  192.2 95.3 %all_to_all.114 = f32[2,128,4096]{1,0,2:T(2,128)S(1)} all-to-all(f32[2,128,4096]{1,0,2:T(2,128)S(1)} %pad_maximum_fusion.1), channel_id=1, replica_groups=mesh['rows'=8,'cols'=4] {'cols'}, dimensions={2} | all-to-all | bytes 8388608 | tf_op jit(solution)/shard_map/all_to_all | solution.py:66
  289.8 5.4 copy.163
  295.2 7.3 copy.164
  302.5 52.9 %all_to_all.115 = f32[2,1024,512]{2,0,1:T(2,128)S(1)} all-to-all(f32[2,1024,512]{2,0,1:T(2,128)} %copy.164), channel_id=1, replica_groups=mesh['rows'=8,'cols'=4] {'rows'}, dimensions={1} | all-to-all | bytes 8388608 | tf_op jit(solution)/shard_map/all_to_all | solution.py:68
  362.6 10.3 %fusion.59 = f32[128,8,512]{2,0,1:T(8,128)} fusion(f32[128,512,8]{1,0,2:T(8,128)} %copy.167), kind=kOutput, calls=%fused_computation.85 | convolution fusion | flops 3224895488 | bytes 4194304 | tf_op jit(solution)/shard_map/rnm,nk->rmk/dot_general | solution.py:38
  372.9 8.4 fusion.71
  385.0 9.9 %convolution_subtract_fusion.1 = f32[128,8,512]{2,0,1:T(8,128)S(1)} fusion(f32[128,8,512]{2,0,1:T(8,128)} %fusion.71, f32[128,512,8]{1,0,2:T(8,128)S(1)} %copy.169), kind=kOutput, calls=%fused_computation.71 | convolution fusion | flops 3225419776 | bytes 6291456 | tf_op jit(solution)/shard_map/rnm,nk->rmk/dot_general | solution.py:38
  395.0 9.2 %multiply_subtract_fusion.2 = (f32[128,8,512]{2,0,1:T(8,128)S(1)}, f32[128,8,512]{2,0,1:T(8,128)S(1)}) fusion(f32[128,8,512]{2,0,1:T(8,128)S(1)} %convolution_subtract_fusion.1, f32[8,512]{1,0:T(8,128)S(1)} %get-tuple-element.32, f32[8,512]{1,0:T(8,128)S(1)} %get-tuple-element.33, f32[128,8,512]{2,0,1:T(8,128)S(1)} %copy-done.9, f32[128,512,8]{1,0,2:T(8,128)S(1)} %copy.169), kind=kOutput, calls=%fused_computation.37 | convolution fusion | flops 3228565504 | bytes 10518528 | tf_op jit(solution)/shard_map/rnm,nk->rmk/dot_general | solution.py:38
  411.8 3.9 all-to-all-start.3
  415.8 22.7 %fusion = f32[1,512,1024]{2,0,1:T(1,128)} fusion(bf16[16,512,1024]{2,1,0:T(8,128)(2,1)} %param.9, f32[16]{0:T(128)S(1)} %copy-done.18), kind=kOutput, calls=%fused_computation.1 | convolution fusion | flops 100663296 | bytes 18874432 | tf_op jit(solution)/shard_map/j,jrc->rc/dot_general | solution.py:92
  438.4 3.9 all-to-all-done.3
  444.5 3.1 multiply_reduce_fusion.1
  449.1 48.1 %all_to_all.116 = f32[1,512,1024]{2,0,1:T(1,128)S(1)} all-to-all(f32[1,512,1024]{2,0,1:T(1,128)S(1)} %broadcast_in_dim.2), channel_id=1, replica_groups=mesh['rows'=8,'cols'=4] {'cols'}, dimensions={1} | all-to-all | bytes 4194304 | tf_op jit(solution)/shard_map/all_to_all | solution.py:72
  501.4 8.4 fusion.68
  509.8 9.0 %multiply_subtract_fusion.1 = (f32[128,8,512]{2,0,1:T(8,128)S(1)}, f32[128,8,512]{2,0,1:T(8,128)S(1)}) fusion(f32[128,8,512]{2,0,1:T(8,128)S(1)} %fusion.68, f32[8,512]{1,0:T(8,128)S(1)} %get-tuple-element.32, f32[8,512]{1,0:T(8,128)S(1)} %get-tuple-element.33, f32[128,512,8]{1,0,2:T(8,128)S(1)} %copy.177), kind=kOutput, calls=%fused_computation.33 | convolution fusion | flops 3228041216 | bytes 8421376 | tf_op jit(solution)/shard_map/rnm,nk->rmk/dot_general | solution.py:38
  527.5 4.3 add_bitcast_fusion.1
  531.7 3.1 copy.213
  536.7 5.3 pad_maximum_fusion.2
  542.0 94.5 %all_to_all.117 = f32[2,128,4096]{1,0,2:T(2,128)S(1)} all-to-all(f32[2,128,4096]{1,0,2:T(2,128)S(1)} %pad_maximum_fusion.2), channel_id=1, replica_groups=mesh['rows'=8,'cols'=4] {'cols'}, dimensions={2} | all-to-all | bytes 8388608 | tf_op jit(solution)/shard_map/all_to_all | solution.py:66
  638.8 5.4 copy.186
  644.2 7.3 copy.187
  651.5 54.8 %all_to_all.118 = f32[2,1024,512]{2,0,1:T(2,128)S(1)} all-to-all(f32[2,1024,512]{2,0,1:T(2,128)} %copy.187), channel_id=1, replica_groups=mesh['rows'=8,'cols'=4] {'rows'}, dimensions={1} | all-to-all | bytes 8388608 | tf_op jit(solution)/shard_map/all_to_all | solution.py:68
  713.5 10.3 %fusion.54 = f32[128,8,512]{2,0,1:T(8,128)} fusion(f32[128,512,8]{1,0,2:T(8,128)} %copy.190), kind=kOutput, calls=%fused_computation.80 | convolution fusion | flops 3224895488 | bytes 4194304 | tf_op jit(solution)/shard_map/rnm,nk->rmk/dot_general | solution.py:38
  723.8 8.4 fusion.66
  736.0 9.9 %convolution_subtract_fusion = f32[128,8,512]{2,0,1:T(8,128)S(1)} fusion(f32[128,8,512]{2,0,1:T(8,128)} %fusion.66, f32[128,512,8]{1,0,2:T(8,128)S(1)} %copy.192), kind=kOutput, calls=%fused_computation.69 | convolution fusion | flops 3225419776 | bytes 6291456 | tf_op jit(solution)/shard_map/rnm,nk->rmk/dot_general | solution.py:38
  745.9 9.2 %multiply_subtract_fusion = (f32[128,8,512]{2,0,1:T(8,128)S(1)}, f32[128,8,512]{2,0,1:T(8,128)S(1)}) fusion(f32[128,8,512]{2,0,1:T(8,128)S(1)} %convolution_subtract_fusion, f32[8,512]{1,0:T(8,128)S(1)} %get-tuple-element.32, f32[8,512]{1,0:T(8,128)S(1)} %get-tuple-element.33, f32[128,8,512]{2,0,1:T(8,128)S(1)} %copy-done.7, f32[128,512,8]{1,0,2:T(8,128)S(1)} %copy.192), kind=kOutput, calls=%fused_computation.29 | convolution fusion | flops 3228565504 | bytes 10518528 | tf_op jit(solution)/shard_map/rnm,nk->rmk/dot_general | solution.py:38
  763.8 4.3 add_bitcast_fusion
  768.1 3.1 copy.215
  773.0 6.8 pad_maximum_fusion.3
  779.8 4.7 all-to-all-start.7
  784.5 7.5 multiply_reduce_fusion
  792.0 41.6 %all-to-all-done.7 = f32[2,128,4096]{1,0,2:T(2,128)} async-done(((f32[2,128,4096]{1,0,2:T(2,128)}), f32[2,128,4096]{1,0,2:T(2,128)}, u32[]{:S(2)}, u32[]{:S(2)}) %all-to-all-start.7) | async-done | bytes 4194336 | tf_op jit(solution)/shard_map/all_to_all | solution.py:76
  833.6 3.9 broadcast_multiply_fusion
  837.6 4.4 copy.274
  842.0 5.0 mul.767
  847.0 6.2 fusion.5
  854.6 38.0 %all-reduce = (f32[16]{0:T(128)S(1)}, f32[]{:T(128)}) all-reduce(f32[16]{0:T(128)S(1)} %multiply_reduce_fusion, f32[]{:T(128)S(6)} %add.265), channel_id=1, replica_groups=mesh['rows'=8,'cols'=4] {'rows','cols'}, use_global_device_ids=true, to_apply=%region_0.1 | all-reduce | flops 17 | bytes 136 | tf_op jit(solution)/shard_map/psum | solution.py:103
  (85 shorter events, 92.7 us)
Async XLA Ops:
  3.9 4.5 copy-start.16
  4.0 4.5 copy-start.14
  17.9 99.9 %all-to-all-start = ((f32[2,512,1024]{2,0,1:T(2,128)}), f32[2,512,1024]{2,0,1:T(2,128)}, u32[]{:S(2)}, u32[]{:S(2)}) async-start(f32[2,512,1024]{2,0,1:T(2,128)} %pad_maximum_fusion), calls=%async_computation | async-start | bytes 8388608 | tf_op jit(solution)/shard_map/all_to_all | solution.py:72
  127.4 10.3 %copy-start.10 = (f32[128,512,8]{1,0,2:T(8,128)S(1)}, f32[128,512,8]{1,0,2:T(8,128)}, u32[]{:S(2)}) copy-start(f32[128,512,8]{1,0,2:T(8,128)} %copy.151) | copy-start | bytes 6291460
  137.6 8.4 copy-start.3
  149.8 10.0 %copy-start.8 = (f32[128,8,512]{2,0,1:T(8,128)S(1)}, f32[128,8,512]{2,0,1:T(8,128)}, u32[]{:S(2)}) copy-start(f32[128,8,512]{2,0,1:T(8,128)} %fusion.62) | copy-start | bytes 6291460
  362.6 10.3 %copy-start.11 = (f32[128,512,8]{1,0,2:T(8,128)S(1)}, f32[128,512,8]{1,0,2:T(8,128)}, u32[]{:S(2)}) copy-start(f32[128,512,8]{1,0,2:T(8,128)} %copy.167) | copy-start | bytes 6291460
  372.9 8.4 copy-start.4
  385.0 10.0 %copy-start.9 = (f32[128,8,512]{2,0,1:T(8,128)S(1)}, f32[128,8,512]{2,0,1:T(8,128)}, u32[]{:S(2)}) copy-start(f32[128,8,512]{2,0,1:T(8,128)} %fusion.59) | copy-start | bytes 6291460
  411.8 3.9 copy-start.18
  411.8 30.5 %all-to-all-start.3 = ((f32[1,128,4096]{1,0,2:T(1,128)}), f32[1,128,4096]{1,0,2:T(1,128)S(1)}, u32[]{:S(2)}, u32[]{:S(2)}) async-start(f32[1,128,4096]{1,0,2:T(1,128)} %bitcast.209), calls=%async_computation.3 | async-start | bytes 4194304 | tf_op jit(solution)/shard_map/all_to_all | solution.py:76
  442.3 2.1 copy-start.6
  442.3 2.2 copy-start.13
  447.6 1.4 copy-start
  713.5 10.3 %copy-start.12 = (f32[128,512,8]{1,0,2:T(8,128)S(1)}, f32[128,512,8]{1,0,2:T(8,128)}, u32[]{:S(2)}) copy-start(f32[128,512,8]{1,0,2:T(8,128)} %copy.190) | copy-start | bytes 6291460
  723.8 8.4 copy-start.5
  736.0 10.0 %copy-start.7 = (f32[128,8,512]{2,0,1:T(8,128)S(1)}, f32[128,8,512]{2,0,1:T(8,128)}, u32[]{:S(2)}) copy-start(f32[128,8,512]{2,0,1:T(8,128)} %fusion.54) | copy-start | bytes 6291460
  779.8 4.7 copy-start.1
  779.8 53.8 %all-to-all-start.7 = ((f32[2,128,4096]{1,0,2:T(2,128)}), f32[2,128,4096]{1,0,2:T(2,128)}, u32[]{:S(2)}, u32[]{:S(2)}) async-start(f32[2,128,4096]{1,0,2:T(2,128)} %pad_maximum_fusion.3), calls=%async_computation.7 | async-start | bytes 8388608 | tf_op jit(solution)/shard_map/all_to_all | solution.py:76
  842.0 5.0 copy-start.2
  842.0 5.0 copy-start.15
  842.0 5.0 copy-start.17
where the time goes:
time: 906 us; the launch traced here: 897 us
  blocking collectives  384 us (42%)
  matrix products  198 us (22%)
  waiting for transfers between devices  139 us (15%)
  local copies, waits for them, and re-layouts  102 us (11%)
  other arithmetic  51.1 us (6%)
  starting transfers between devices  15.1 us (2%)
    all_to_all x2, blocking collectives, middle_step(): lax.all_to_all(spread, 'cols', split_axis=2, concat_axis=1, tiled=True)  190 us
    dot_general x14, matrix products, apply_big(): return jnp.einsum('rnm,nk->rmk', block, table, precision=highest)  131 us
    all_to_all x2, blocking collectives, middle_step(): lax.all_to_all(flipped, 'rows', split_axis=1, concat_axis=2, tiled=True)  108 us
    all_to_all x1, waiting for transfers between devices, grid_transform(): lax.all_to_all(pieces, 'cols', split_axis=1, concat_axis=2, tiled=True)  93.3 us
    all_to_all x1, blocking collectives, grid_transform(): lax.all_to_all(pieces, 'cols', split_axis=1, concat_axis=2, tiled=True)  48.1 us
    all_to_all x2, waiting for transfers between devices, grid_transform(): lax.all_to_all(second, 'rows', split_axis=2, concat_axis=1, tiled=True)  45.5 us
    dot_general x14, matrix products, apply_small(): return jnp.einsum('rmk,mj->rjk', block, table, precision=highest)  44.6 us
    psum x1, blocking collectives, shards(): lax.psum((partial_coef, partial_loss), ('rows', 'cols'))  38 us
  transfers between devices with their start and end apart: 3, of which 3 were waited for; matrix products, arithmetic and copies ran while one was open for 3% of the time, Pallas kernels for 0%

commit v1 on v0

--- a/solution.py
+++ b/solution.py
@@ -7,6 +7,22 @@
 NG = 4096
 lasso_weight = 0.02
 ridge_weight = 0.1
+
+
+def exchange_in_pairs(value, axis, split, join):
+    ways, here = (lax.axis_size(axis), lax.axis_index(axis))
+    width = value.shape[split] // ways
+    dims = list(value.shape)
+    dims[split] = width
+    height = dims[join]
+    dims[join] = height * ways
+    full = jnp.zeros(dims, value.dtype)
+    for mask in range(ways):
+        part = lax.dynamic_slice_in_dim(value, (here ^ mask) * width, width, axis=split)
+        if mask:
+            part = lax.ppermute(part, axis, [(d, d ^ mask) for d in range(ways)])
+        full = lax.dynamic_update_slice_in_dim(full, part, (here ^ mask) * height, axis=join)
+    return full
 
 
 def field_spectrum(field_hyper, wave_row, wave_col):
@@ -73,7 +89,7 @@
     halfway = inverse_transform(full_rows, False)
     columns = middle_step(halfway)
     second = inverse_transform(columns, want_real)
-    blocks_out = lax.all_to_all(second, "rows", split_axis=2, concat_axis=1, tiled=True)
+    blocks_out = exchange_in_pairs(second, "rows", 2, 1)
     return jnp.swapaxes(blocks_out, 1, 2) * (1.0 / NG)
 
 

time: 906 us -> 935 us (1.032)
  waiting for transfers between devices: 139 us -> 197 us
  blocking collectives: 384 us -> 333 us
  matrix products: 198 us -> 216 us
  other arithmetic: 51.1 us -> 38.9 us
    all_to_all x2 -> x1, blocking collectives: 108 us -> 52.8 us  [middle_step(): lax.all_to_all(flipped, 'rows', split_axis=1, concat_axis=2, tiled=True)]
    ppermute x0 -> x14, waiting for transfers between devices: none -> 54.4 us  [exchange_in_pairs(): part = lax.ppermute(part, axis, [(d, d ^ mask) for d in range(ways)])]
    dot_general x14, matrix products: 44.6 us -> 57.2 us  [apply_small(): return jnp.einsum('rmk,mj->rjk', block, table, precision=highest)]
    ppermute x0 -> x14, starting transfers between devices: none -> 10.6 us  [exchange_in_pairs(): part = lax.ppermute(part, axis, [(d, d ^ mask) for d in range(ways)])]
    mul x2 -> x0, local copies, waits for them, and re-layouts: 9.44 us -> none  [grid_transform(): return jnp.swapaxes(blocks_out, 1, 2) * (1.0 / NG)]
    all_to_all x2 -> x1, waiting for transfers between devices: 45.5 us -> 49.1 us  [middle_step(): lax.all_to_all(flipped, 'rows', split_axis=1, concat_axis=2, tiled=True)]
  transfers between devices with their start and end apart: 3 -> 16, of which waited for: 3 -> 7; matrix products, arithmetic and copies ran while one was open for 3% -> 4% of each run, Pallas kernels for 0% -> 0%
where the time goes in v1:
time: 935 us; the launch traced here: 926 us
  blocking collectives  333 us (36%)
  matrix products  216 us (23%)
  waiting for transfers between devices  197 us (21%)
  local copies, waits for them, and re-layouts  110 us (12%)
  other arithmetic  38.9 us (4%)
  starting transfers between devices  21.8 us (2%)
    all_to_all x2, blocking collectives, middle_step(): lax.all_to_all(spread, 'cols', split_axis=2, concat_axis=1, tiled=True)  191 us
    dot_general x14, matrix products, apply_big(): return jnp.einsum('rnm,nk->rmk', block, table, precision=highest)  136 us
    all_to_all x1, waiting for transfers between devices, grid_transform(): lax.all_to_all(pieces, 'cols', split_axis=1, concat_axis=2, tiled=True)  93.3 us
    dot_general x14, matrix products, apply_small(): return jnp.einsum('rmk,mj->rjk', block, table, precision=highest)  57.2 us
    ppermute x14, waiting for transfers between devices, exchange_in_pairs(): part = lax.ppermute(part, axis, [(d, d ^ mask) for d in range(ways)])  54.4 us
    all_to_all x1, blocking collectives, middle_step(): lax.all_to_all(flipped, 'rows', split_axis=1, concat_axis=2, tiled=True)  52.8 us
    all_to_all x1, blocking collectives, grid_transform(): lax.all_to_all(pieces, 'cols', split_axis=1, concat_axis=2, tiled=True)  51.6 us
    all_to_all x1, waiting for transfers between devices, middle_step(): lax.all_to_all(flipped, 'rows', split_axis=1, concat_axis=2, tiled=True)  49.1 us
  transfers between devices with their start and end apart: 16, of which 7 were waited for; matrix products, arithmetic and copies ran while one was open for 4% of the time, Pallas kernels for 0%

profile of v1, /device:TPU:0, one launch (start us, length us, event | category | flops | bytes accessed | tf_op | source)
XLA Modules:
  0.0 925.9 jit_solution(12818683819105829969)
XLA Ops:
  4.6 3.8 multiply_bitcast_fusion.1
  12.1 5.8 pad_maximum_fusion
  17.9 6.5 all-to-all-start
  24.5 93.3 %all-to-all-done = f32[2,512,1024]{2,0,1:T(2,128)} async-done(((f32[2,512,1024]{2,0,1:T(2,128)}), f32[2,512,1024]{2,0,1:T(2,128)}, u32[]{:S(2)}, u32[]{:S(2)}) %all-to-all-start) | async-done | bytes 4194336 | tf_op jit(solution)/shard_map/all_to_all | solution.py:88
  127.4 10.3 %fusion.73 = f32[128,8,512]{2,0,1:T(8,128)} fusion(f32[128,512,8]{1,0,2:T(8,128)} %copy.180), kind=kOutput, calls=%fused_computation.113 | convolution fusion | flops 3224895488 | bytes 4194304 | tf_op jit(solution)/shard_map/rnm,nk->rmk/dot_general | solution.py:54
  137.7 8.4 fusion.61
  149.9 10.7 %convolution_subtract_fusion.2 = f32[128,8,512]{2,0,1:T(8,128)S(1)} fusion(f32[128,8,512]{2,0,1:T(8,128)} %fusion.73, f32[128,512,8]{1,0,2:T(8,128)S(1)} %copy.182), kind=kOutput, calls=%fused_computation.86 | convolution fusion | flops 3225419776 | bytes 6291456 | tf_op jit(solution)/shard_map/rnm,nk->rmk/dot_general | solution.py:54
  160.6 10.6 %multiply_subtract_fusion.3 = (f32[128,8,512]{2,0,1:T(8,128)S(1)}, f32[128,8,512]{2,0,1:T(8,128)S(1)}) fusion(f32[128,8,512]{2,0,1:T(8,128)S(1)} %convolution_subtract_fusion.2, f32[8,512]{1,0:T(8,128)S(1)} %get-tuple-element.48, f32[8,512]{1,0:T(8,128)S(1)} %get-tuple-element.49, f32[128,8,512]{2,0,1:T(8,128)S(1)} %copy-done.16, f32[128,512,8]{1,0,2:T(8,128)} %copy-done.1), kind=kOutput, calls=%fused_computation.54 | convolution fusion | flops 3228565504 | bytes 10518528 | tf_op jit(solution)/shard_map/rnm,nk->rmk/dot_general | solution.py:54
  174.1 4.2 fusion.30
  178.3 4.3 add_bitcast_fusion.2
  186.0 5.8 subtract_bitcast_fusion.3
  194.9 5.0 pad_maximum_fusion.1
  199.8 95.3 %all_to_all.96 = f32[2,128,4096]{1,0,2:T(2,128)S(1)} all-to-all(f32[2,128,4096]{1,0,2:T(2,128)S(1)} %pad_maximum_fusion.1), channel_id=1, replica_groups=mesh['rows'=8,'cols'=4] {'cols'}, dimensions={2} | all-to-all | bytes 8388608 | tf_op jit(solution)/shard_map/all_to_all | solution.py:82
  297.5 5.4 copy.192
  302.9 7.2 copy.193
  310.1 4.7 all-to-all-start.2
  314.9 49.1 %all-to-all-done.2 = f32[2,1024,512]{2,0,1:T(2,128)} async-done(((f32[2,1024,512]{2,0,1:T(2,128)}), f32[2,1024,512]{2,0,1:T(2,128)}, u32[]{:S(2)}, u32[]{:S(2)}) %all-to-all-start.2) | async-done | bytes 4194336 | tf_op jit(solution)/shard_map/all_to_all | solution.py:84
  373.4 10.3 %fusion.70 = f32[128,8,512]{2,0,1:T(8,128)} fusion(f32[128,512,8]{1,0,2:T(8,128)} %copy.196), kind=kOutput, calls=%fused_computation.110 | convolution fusion | flops 3224895488 | bytes 4194304 | tf_op jit(solution)/shard_map/rnm,nk->rmk/dot_general | solution.py:54
  383.7 8.4 fusion.58
  395.9 9.9 %convolution_subtract_fusion.1 = f32[128,8,512]{2,0,1:T(8,128)S(1)} fusion(f32[128,8,512]{2,0,1:T(8,128)} %fusion.70, f32[128,512,8]{1,0,2:T(8,128)S(1)} %copy.198), kind=kOutput, calls=%fused_computation.84 | convolution fusion | flops 3225419776 | bytes 6291456 | tf_op jit(solution)/shard_map/rnm,nk->rmk/dot_general | solution.py:54
  405.8 9.0 multiply_subtract_fusion.2
  426.9 23.3 %fusion = f32[1,512,1024]{2,0,1:T(1,128)} fusion(bf16[16,512,1024]{2,1,0:T(8,128)(2,1)} %param.9, f32[16]{0:T(128)S(1)} %copy-done.26), kind=kOutput, calls=%fused_computation.1 | convolution fusion | flops 100663296 | bytes 18874432 | tf_op jit(solution)/shard_map/j,jrc->rc/dot_general | solution.py:108
  457.7 12.9 %collective-permute-done.3 = f32[1,128,512]{1,2,0:T(8,128)S(1)} collective-permute-done((f32[1,128,512]{1,2,0:T(8,128)S(1)}, f32[1,128,512]{1,2,0:T(8,128)S(1)}, u32[]{:S(2)}, u32[]{:S(2)}) %collective-permute-start.3) | collective-permute-done | bytes 262176 | tf_op jit(solution)/shard_map/ppermute | solution.py:23
  470.7 4.3 collective-permute-done.4
  475.1 3.9 multiply_reduce_fusion.1
  480.5 51.6 %all_to_all.97 = f32[1,512,1024]{2,0,1:T(1,128)S(1)} all-to-all(f32[1,512,1024]{2,0,1:T(1,128)S(1)} %broadcast_in_dim.8), channel_id=1, replica_groups=mesh['rows'=8,'cols'=4] {'cols'}, dimensions={1} | all-to-all | bytes 4194304 | tf_op jit(solution)/shard_map/all_to_all | solution.py:88
  537.6 8.4 fusion.67
  546.0 10.5 %multiply_subtract_fusion.1 = (f32[128,8,512]{2,0,1:T(8,128)S(1)}, f32[128,8,512]{2,0,1:T(8,128)S(1)}) fusion(f32[128,8,512]{2,0,1:T(8,128)S(1)} %fusion.67, f32[8,512]{1,0:T(8,128)S(1)} %get-tuple-element.48, f32[8,512]{1,0:T(8,128)S(1)} %get-tuple-element.49, f32[128,512,8]{1,0,2:T(8,128)} %copy-done.18), kind=kOutput, calls=%fused_computation.46 | convolution fusion | flops 3228041216 | bytes 8421376 | tf_op jit(solution)/shard_map/rnm,nk->rmk/dot_general | solution.py:54
  559.3 4.2 fusion.22
  563.6 4.3 add_bitcast_fusion.1
  570.8 5.8 subtract_bitcast_fusion.1
  579.7 5.0 pad_maximum_fusion.2
  584.7 95.7 %all_to_all.98 = f32[2,128,4096]{1,0,2:T(2,128)S(1)} all-to-all(f32[2,128,4096]{1,0,2:T(2,128)S(1)} %pad_maximum_fusion.2), channel_id=1, replica_groups=mesh['rows'=8,'cols'=4] {'cols'}, dimensions={2} | all-to-all | bytes 8388608 | tf_op jit(solution)/shard_map/all_to_all | solution.py:82
  682.6 5.4 copy.221
  688.0 7.2 copy.222
  695.2 52.8 %all_to_all.99 = f32[2,1024,512]{2,0,1:T(2,128)S(1)} all-to-all(f32[2,1024,512]{2,0,1:T(2,128)} %copy.222), channel_id=1, replica_groups=mesh['rows'=8,'cols'=4] {'rows'}, dimensions={1} | all-to-all | bytes 8388608 | tf_op jit(solution)/shard_map/all_to_all | solution.py:84
  755.4 10.3 %fusion.65 = f32[128,8,512]{2,0,1:T(8,128)} fusion(f32[128,512,8]{1,0,2:T(8,128)} %copy.225), kind=kOutput, calls=%fused_computation.105 | convolution fusion | flops 3224895488 | bytes 4194304 | tf_op jit(solution)/shard_map/rnm,nk->rmk/dot_general | solution.py:54
  765.6 8.4 fusion.53
  779.1 9.9 %convolution_subtract_fusion = f32[128,8,512]{2,0,1:T(8,128)S(1)} fusion(f32[128,8,512]{2,0,1:T(8,128)} %fusion.65, f32[128,512,8]{1,0,2:T(8,128)S(1)} %copy.227), kind=kOutput, calls=%fused_computation.82 | convolution fusion | flops 3225419776 | bytes 6291456 | tf_op jit(solution)/shard_map/rnm,nk->rmk/dot_general | solution.py:54
  789.0 10.7 %multiply_subtract_fusion = (f32[128,8,512]{2,0,1:T(8,128)S(1)}, f32[128,8,512]{2,0,1:T(8,128)S(1)}) fusion(f32[128,8,512]{2,0,1:T(8,128)S(1)} %convolution_subtract_fusion, f32[8,512]{1,0:T(8,128)S(1)} %get-tuple-element.48, f32[8,512]{1,0:T(8,128)S(1)} %get-tuple-element.49, f32[128,8,512]{2,0,1:T(8,128)S(1)} %copy-done.15, f32[128,512,8]{1,0,2:T(8,128)} %copy-done), kind=kOutput, calls=%fused_computation.42 | convolution fusion | flops 3228565504 | bytes 10518528 | tf_op jit(solution)/shard_map/rnm,nk->rmk/dot_general | solution.py:54
  802.7 4.2 fusion.12
  806.9 4.2 subtract_bitcast_fusion
  814.2 5.8 add_bitcast_fusion
  829.8 7.5 multiply_reduce_fusion
  841.1 10.3 %collective-permute-done.9 = f32[2,128,512]{1,2,0:T(8,128)S(1)} collective-permute-done((f32[2,128,512]{1,2,0:T(8,128)S(1)}, f32[2,128,512]{1,2,0:T(8,128)S(1)}, u32[]{:S(2)}, u32[]{:S(2)}) %collective-permute-start.9) | collective-permute-done | bytes 524320 | tf_op jit(solution)/shard_map/ppermute | solution.py:23
  851.5 23.9 %collective-permute-done.11 = f32[2,128,512]{1,2,0:T(8,128)S(1)} collective-permute-done((f32[2,128,512]{1,2,0:T(8,128)S(1)}, f32[2,128,512]{1,2,0:T(8,128)S(1)}, u32[]{:S(2)}, u32[]{:S(2)}) %collective-permute-start.11) | collective-permute-done | bytes 524320 | tf_op jit(solution)/shard_map/ppermute | solution.py:23
  877.9 4.3 fusion.4
  883.4 38.0 %all-reduce = (f32[16]{0:T(128)S(1)}, f32[]{:T(128)}) all-reduce(f32[16]{0:T(128)S(1)} %multiply_reduce_fusion, f32[]{:T(128)S(6)} %add.345), channel_id=1, replica_groups=mesh['rows'=8,'cols'=4] {'rows','cols'}, use_global_device_ids=true, to_apply=%region_0.1 | all-reduce | flops 17 | bytes 136 | tf_op jit(solution)/shard_map/psum | solution.py:119
  (141 shorter events, 116.6 us)
Async XLA Ops:
  3.3 5.2 copy-start.22
  3.3 5.2 copy-start.24
  17.9 99.9 %all-to-all-start = ((f32[2,512,1024]{2,0,1:T(2,128)}), f32[2,512,1024]{2,0,1:T(2,128)}, u32[]{:S(2)}, u32[]{:S(2)}) async-start(f32[2,512,1024]{2,0,1:T(2,128)} %pad_maximum_fusion), calls=%async_computation | async-start | bytes 8388608 | tf_op jit(solution)/shard_map/all_to_all | solution.py:88
  127.4 10.3 %copy-start.19 = (f32[128,512,8]{1,0,2:T(8,128)S(1)}, f32[128,512,8]{1,0,2:T(8,128)}, u32[]{:S(2)}) copy-start(f32[128,512,8]{1,0,2:T(8,128)} %copy.180) | copy-start | bytes 6291460
  137.7 8.4 copy-start.9
  149.8 10.7 %copy-start.1 = (f32[128,512,8]{1,0,2:T(8,128)}, f32[128,512,8]{1,0,2:T(8,128)S(1)}, u32[]{:S(2)}) copy-start(f32[128,512,8]{1,0,2:T(8,128)S(1)} %copy.182) | copy-start | bytes 6291460
  149.9 10.7 %copy-start.16 = (f32[128,8,512]{2,0,1:T(8,128)S(1)}, f32[128,8,512]{2,0,1:T(8,128)}, u32[]{:S(2)}) copy-start(f32[128,8,512]{2,0,1:T(8,128)} %fusion.61) | copy-start | bytes 6291460
  191.7 3.1 copy-start.12
  310.1 53.9 %all-to-all-start.2 = ((f32[2,1024,512]{2,0,1:T(2,128)}), f32[2,1024,512]{2,0,1:T(2,128)}, u32[]{:S(2)}, u32[]{:S(2)}) async-start(f32[2,1024,512]{2,0,1:T(2,128)} %copy.193), calls=%async_computation.2 | async-start | bytes 8388608 | tf_op jit(solution)/shard_map/all_to_all | solution.py:84
  373.4 10.3 %copy-start.20 = (f32[128,512,8]{1,0,2:T(8,128)S(1)}, f32[128,512,8]{1,0,2:T(8,128)}, u32[]{:S(2)}) copy-start(f32[128,512,8]{1,0,2:T(8,128)} %copy.196) | copy-start | bytes 6291460
  383.7 8.4 copy-start.10
  395.9 10.0 %copy-start.17 = (f32[128,8,512]{2,0,1:T(8,128)S(1)}, f32[128,8,512]{2,0,1:T(8,128)}, u32[]{:S(2)}) copy-start(f32[128,8,512]{2,0,1:T(8,128)} %fusion.58) | copy-start | bytes 6291460
  422.5 1.6 copy-start.6
  424.1 2.8 copy-start.26
  425.0 26.9 %collective-permute-start = (f32[1,128,512]{1,2,0:T(8,128)}, f32[1,128,512]{1,2,0:T(8,128)}, u32[]{:S(2)}, u32[]{:S(2)}) collective-permute-start(f32[1,128,512]{1,2,0:T(8,128)} %get-tuple-element.41), channel_id=1, source_target_pairs={{0,4},{4,0},{8,12},{12,8},{16,20},{20,16},{24,28},{28,24},{1,5},{5... | collective-permute-start | bytes 786440 | tf_op jit(solution)/shard_map/ppermute | solution.py:23
  425.0 28.4 %collective-permute-start.1 = (f32[1,128,512]{1,2,0:T(8,128)}, f32[1,128,512]{1,2,0:T(8,128)}, u32[]{:S(2)}, u32[]{:S(2)}) collective-permute-start(f32[1,128,512]{1,2,0:T(8,128)} %get-tuple-element.40), channel_id=1, source_target_pairs={{0,8},{4,12},{8,0},{12,4},{16,24},{20,28},{24,16},{28,20},{1,9},{5... | collective-permute-start | bytes 786440 | tf_op jit(solution)/shard_map/ppermute | solution.py:23
  425.6 31.1 %collective-permute-start.2 = (f32[1,128,512]{1,2,0:T(8,128)S(1)}, f32[1,128,512]{1,2,0:T(8,128)}, u32[]{:S(2)}, u32[]{:S(2)}) collective-permute-start(f32[1,128,512]{1,2,0:T(8,128)S(1)} %get-tuple-element.39), channel_id=1, source_target_pairs={{0,12},{4,8},{8,4},{12,0},{16,28},{20,24},{24,20},{28,16},{1,13},{... | collective-permute-start | bytes 786440 | tf_op jit(solution)/shard_map/ppermute | solution.py:23
  450.2 24.9 %copy-start.14 = (f32[1,512,1024]{2,0,1:T(1,128)S(1)}, f32[1,512,1024]{2,0,1:T(1,128)}, u32[]{:S(2)}) copy-start(f32[1,512,1024]{2,0,1:T(1,128)} %fusion) | copy-start | bytes 6291460
  450.2 20.4 %collective-permute-start.3 = (f32[1,128,512]{1,2,0:T(8,128)S(1)}, f32[1,128,512]{1,2,0:T(8,128)S(1)}, u32[]{:S(2)}, u32[]{:S(2)}) collective-permute-start(f32[1,128,512]{1,2,0:T(8,128)S(1)} %get-tuple-element.38), channel_id=1, source_target_pairs={{0,16},{4,20},{8,24},{12,28},{16,0},{20,4},{24,8},{28,12},{1,17},{... | collective-permute-start | bytes 786440 | tf_op jit(solution)/shard_map/ppermute | solution.py:23
  450.8 24.2 %collective-permute-start.4 = (f32[1,128,512]{1,2,0:T(8,128)S(1)}, f32[1,128,512]{1,2,0:T(8,128)S(1)}, u32[]{:S(2)}, u32[]{:S(2)}) collective-permute-start(f32[1,128,512]{1,2,0:T(8,128)S(1)} %get-tuple-element.37), channel_id=1, source_target_pairs={{0,20},{4,16},{8,28},{12,24},{16,4},{20,0},{24,12},{28,8},{1,21},{... | collective-permute-start | bytes 786440 | tf_op jit(solution)/shard_map/ppermute | solution.py:23
  451.9 23.1 %collective-permute-start.5 = (f32[1,128,512]{1,2,0:T(8,128)S(1)}, f32[1,128,512]{1,2,0:T(8,128)S(1)}, u32[]{:S(2)}, u32[]{:S(2)}) collective-permute-start(f32[1,128,512]{1,2,0:T(8,128)S(1)} %get-tuple-element.36), channel_id=1, source_target_pairs={{0,24},{4,28},{8,16},{12,20},{16,8},{20,12},{24,0},{28,4},{1,25},{... | collective-permute-start | bytes 786440 | tf_op jit(solution)/shard_map/ppermute | solution.py:23
  453.5 21.6 %collective-permute-start.6 = (f32[1,128,512]{1,2,0:T(8,128)S(1)}, f32[1,128,512]{1,2,0:T(8,128)S(1)}, u32[]{:S(2)}, u32[]{:S(2)}) collective-permute-start(f32[1,128,512]{1,2,0:T(8,128)S(1)} %get-tuple-element.35), channel_id=1, source_target_pairs={{0,28},{4,24},{8,20},{12,16},{16,12},{20,8},{24,4},{28,0},{1,29},{... | collective-permute-start | bytes 786440 | tf_op jit(solution)/shard_map/ppermute | solution.py:23
  479.0 1.4 copy-start.4
  536.3 1.3 copy-start.18
  576.5 3.1 copy-start.13
  755.4 10.3 %copy-start.21 = (f32[128,512,8]{1,0,2:T(8,128)S(1)}, f32[128,512,8]{1,0,2:T(8,128)}, u32[]{:S(2)}) copy-start(f32[128,512,8]{1,0,2:T(8,128)} %copy.225) | copy-start | bytes 6291460
  765.6 8.4 copy-start.11
  777.8 1.3 copy-start
  779.1 9.9 %copy-start.15 = (f32[128,8,512]{2,0,1:T(8,128)S(1)}, f32[128,8,512]{2,0,1:T(8,128)}, u32[]{:S(2)}) copy-start(f32[128,8,512]{2,0,1:T(8,128)} %fusion.53) | copy-start | bytes 6291460
  820.0 3.1 copy-start.2
  824.4 1.6 copy-start.3
  825.9 3.9 copy-start.5
  826.2 11.2 %collective-permute-start.7 = (f32[2,128,512]{1,2,0:T(8,128)S(1)}, f32[2,128,512]{1,2,0:T(8,128)S(1)}, u32[]{:S(2)}, u32[]{:S(2)}) collective-permute-start(f32[2,128,512]{1,2,0:T(8,128)S(1)} %get-tuple-element.23), channel_id=1, source_target_pairs={{0,4},{4,0},{8,12},{12,8},{16,20},{20,16},{24,28},{28,24},{1,5},{5... | collective-permute-start | bytes 1572872 | tf_op jit(solution)/shard_map/ppermute | solution.py:23
  826.2 14.8 %collective-permute-start.8 = (f32[2,128,512]{1,2,0:T(8,128)S(1)}, f32[2,128,512]{1,2,0:T(8,128)S(1)}, u32[]{:S(2)}, u32[]{:S(2)}) collective-permute-start(f32[2,128,512]{1,2,0:T(8,128)S(1)} %get-tuple-element.24), channel_id=1, source_target_pairs={{0,8},{4,12},{8,0},{12,4},{16,24},{20,28},{24,16},{28,20},{1,9},{5... | collective-permute-start | bytes 1572872 | tf_op jit(solution)/shard_map/ppermute | solution.py:23
  826.9 24.5 %collective-permute-start.9 = (f32[2,128,512]{1,2,0:T(8,128)S(1)}, f32[2,128,512]{1,2,0:T(8,128)S(1)}, u32[]{:S(2)}, u32[]{:S(2)}) collective-permute-start(f32[2,128,512]{1,2,0:T(8,128)S(1)} %get-tuple-element.25), channel_id=1, source_target_pairs={{0,12},{4,8},{8,4},{12,0},{16,28},{20,24},{24,20},{28,16},{1,13},{... | collective-permute-start | bytes 1572872 | tf_op jit(solution)/shard_map/ppermute | solution.py:23
  828.1 23.3 %collective-permute-start.10 = (f32[2,128,512]{1,2,0:T(8,128)S(1)}, f32[2,128,512]{1,2,0:T(8,128)S(1)}, u32[]{:S(2)}, u32[]{:S(2)}) collective-permute-start(f32[2,128,512]{1,2,0:T(8,128)S(1)} %get-tuple-element.27), channel_id=1, source_target_pairs={{0,16},{4,20},{8,24},{12,28},{16,0},{20,4},{24,8},{28,12},{1,17},{... | collective-permute-start | bytes 1572872 | tf_op jit(solution)/shard_map/ppermute | solution.py:23
  828.7 46.8 %collective-permute-start.11 = (f32[2,128,512]{1,2,0:T(8,128)S(1)}, f32[2,128,512]{1,2,0:T(8,128)S(1)}, u32[]{:S(2)}, u32[]{:S(2)}) collective-permute-start(f32[2,128,512]{1,2,0:T(8,128)S(1)} %get-tuple-element.28), channel_id=1, source_target_pairs={{0,20},{4,16},{8,28},{12,24},{16,4},{20,0},{24,12},{28,8},{1,21},{... | collective-permute-start | bytes 1572872 | tf_op jit(solution)/shard_map/ppermute | solution.py:23
  837.4 38.1 %collective-permute-start.12 = (f32[2,128,512]{1,2,0:T(8,128)S(1)}, f32[2,128,512]{1,2,0:T(8,128)S(1)}, u32[]{:S(2)}, u32[]{:S(2)}) collective-permute-start(f32[2,128,512]{1,2,0:T(8,128)S(1)} %get-tuple-element.26), channel_id=1, source_target_pairs={{0,24},{4,28},{8,16},{12,20},{16,8},{20,12},{24,0},{28,4},{1,25},{... | collective-permute-start | bytes 1572872 | tf_op jit(solution)/shard_map/ppermute | solution.py:23
  841.0 34.5 %collective-permute-start.13 = (f32[2,128,512]{1,2,0:T(8,128)S(1)}, f32[2,128,512]{1,2,0:T(8,128)S(1)}, u32[]{:S(2)}, u32[]{:S(2)}) collective-permute-start(f32[2,128,512]{1,2,0:T(8,128)S(1)} %get-tuple-element.21), channel_id=1, source_target_pairs={{0,28},{4,24},{8,20},{12,16},{16,12},{20,8},{24,4},{28,0},{1,29},{... | collective-permute-start | bytes 1572872 | tf_op jit(solution)/shard_map/ppermute | solution.py:23
  875.7 1.6 copy-start.7
  875.7 2.2 copy-start.8
  875.7 2.2 copy-start.23
  875.7 2.2 copy-start.25
